TPU v7x, 256 devices: a whole 4x4x8 slice. The times are simulated.
256 devices in a mesh: grp: 4 (over z_hi), gx: 32 (over x, y, core), gy: 2 (over z_lo).
Axes of the slice: x: 4, y: 4, z: 8 (z_hi: 4, z_lo: 2; z = z_hi * 2 + z_lo), core: 2. Of those that a mesh axis runs over, the one named last changes fastest.
Arguments:
- state: float32 [8, 4, 125, 32, 256], P(('grp', 'gy'), None, None, 'gx'), may hold values from -6 to 6
- damping: float32 [32, 256], P('gx'), may hold values from 0.5 to 20
- absorb_mask: int32 [32, 256], P('gx'), may hold values 0 or 1
- lift_gain: float32 [64], replicated, may hold values from -3 to 3
- proj_weight: float32 [64], replicated, may hold values from -0.75 to 0.75
- spectral: float32 [4096, 64, 64], P('gx'), may hold values from -3 to 3
- moment_one: bfloat16 [4096, 64, 64], P('gx'), may hold values from -5 to 5
- moment_two: bfloat16 [4096, 64, 64], P('gx'), may hold values from 0.0099487305 to 1
Outputs:
- new_state: float32 [8, 4, 125, 32, 256], P(('grp', 'gy'), None, None, 'gx')
- new_spectral: float32 [4096, 64, 64], P('gx')
- new_moment_one: bfloat16 [4096, 64, 64], P('gx')
- new_moment_two: bfloat16 [4096, 64, 64], P('gx')
All inputs are finite; a program needn't handle non-finite values. No bound on the sum of `absorb_mask` on one device may be relied on, other than what follows from the above.
Results may differ from a plain program's by a relative error of at most 0.0004.
Values may be sent and summed in bfloat16 or wider, within the bound.
A program may use at most 64 MiB of HBM per device.

v0:
```python
import math

import jax
import jax.numpy as jnp
import numpy as np
from jax import lax
from jax.experimental import pallas as pl
from jax.experimental.pallas import tpu as pltpu
from jax.sharding import PartitionSpec as P

MESH = pl.DeviceIdType.MESH
HIGHEST = lax.Precision.HIGHEST
KM = 16
CHIPS = 16
ZPEERS = 8
TIME_STEP = 0.02
FACE_GAIN = 10.0
LOSS_SCALE = 1.0 / 2048.0
LEARN_RATE = 0.001
BETA_ONE = 0.9
BETA_TWO = 0.999
BIAS_ONE = 1.0 - BETA_ONE**10
BIAS_TWO = 1.0 - BETA_TWO**10
EPSILON = 1e-08
HALF_ROOT = 1.0 / math.sqrt(2.0)
GAUSS_NORM = 1.0 / math.sqrt(2.0 * math.pi)
LOG2E = 1.4426950408889634


def lagrange(nodes, column, point):
    value = 1.0
    for other in range(len(nodes)):
        if other != column:
            value = value * (point - nodes[other]) / (nodes[column] - nodes[other])
    return value


def lagrange_slope(nodes, column, point):
    total = 0.0
    for skipped in range(len(nodes)):
        if skipped != column:
            factor = 1.0 / (nodes[column] - nodes[skipped])
            for other in range(len(nodes)):
                if other != column and other != skipped:
                    factor = factor * (point - nodes[other]) / (nodes[column] - nodes[other])
            total = total + factor
    return total


def gll_tables():
    nodes = [-1.0, -math.sqrt(3.0 / 7.0), 0.0, math.sqrt(3.0 / 7.0), 1.0]
    slopes = np.array([[lagrange_slope(nodes, c, nodes[r]) for c in range(5)] for r in range(5)])
    interp = np.array(
        [[lagrange(nodes, c, -1.0 + (2.0 * m + 1.0) / 4.0) for c in range(5)] for m in range(4)]
    )
    return slopes.astype(np.float32), interp.astype(np.float32)


def fourier_table(length, kept):
    angles = np.arange(length) * (2.0 * math.pi / length)
    rows = []
    for freq in range(kept // 2 + 1):
        factor = math.sqrt(1.0 / length) if freq == 0 else math.sqrt(2.0 / length)
        rows.append(factor * np.cos(freq * angles))
    for freq in range(1, kept // 2):
        rows.append(math.sqrt(2.0 / length) * np.sin(freq * angles))
    return np.stack(rows)


def node_of(index, axis, value):
    out = list(index)
    out[axis] = value
    return 25 * out[0] + 5 * out[1] + out[2]


def solver_tables(slopes):
    own = np.zeros((512, 512))
    near = np.zeros((512, 192))
    pick = np.zeros((192, 512))
    for i1 in range(5):
        for i2 in range(5):
            for i3 in range(5):
                index = (i1, i2, i3)
                node = 25 * i1 + 5 * i2 + i3
                for d in range(3):
                    u = 125 * (1 + d)
                    for k in range(5):
                        other = node_of(index, d, k)
                        own[node, u + other] += -2.0 * slopes[index[d], k]
                        own[u + node, other] += -2.0 * slopes[index[d], k]
                    rest = [index[e] for e in range(3) if e != d]
                    face = 5 * rest[0] + rest[1]
                    low, high = 64 * d + face, 64 * d + 32 + face
                    if index[d] == 0:
                        own[node, u + node] -= FACE_GAIN
                        own[node, node] -= FACE_GAIN
                        own[u + node, u + node] -= FACE_GAIN
                        own[u + node, node] -= FACE_GAIN
                        near[node, low] = FACE_GAIN
                        near[u + node, low] = FACE_GAIN
                        pick[high, node] = 1.0
                        pick[high, u + node] = -1.0
                    if index[d] == 4:
                        own[node, u + node] += FACE_GAIN
                        own[node, node] -= FACE_GAIN
                        own[u + node, node] += FACE_GAIN
                        own[u + node, u + node] -= FACE_GAIN
                        near[node, high] = FACE_GAIN
                        near[u + node, high] = -FACE_GAIN
                        pick[low, node] = 1.0
                        pick[low, u + node] = 1.0
    return tuple(t.astype(np.float32) for t in (own, near, pick))


def tables():
    slopes, interp = gll_tables()
    own, near, pick = solver_tables(slopes.astype(np.float64))
    interp = interp.astype(np.float64)
    regrid = np.zeros((64, 128), np.float32)
    regrid[:, :125] = np.kron(np.kron(interp, interp), interp).astype(np.float32)
    joint = np.kron(fourier_table(64, KM), fourier_table(64, KM)).astype(np.float32)
    joint = joint.reshape(256, 16, 4, 16, 4).transpose(2, 4, 0, 1, 3).reshape(16, 256, 256)
    inverse = jnp.asarray(joint).astype(jnp.bfloat16)
    forward = jnp.asarray(joint.transpose(0, 2, 1)).astype(jnp.bfloat16)
    along_x = jnp.asarray(fourier_table(128, KM), dtype=jnp.float32).astype(jnp.bfloat16)
    along_x = along_x.astype(jnp.float32).reshape(-1)
    return own, near, pick, regrid, forward, inverse, along_x


def normal_parts(x):
    bell = jnp.exp2(x * x * (-0.5 * LOG2E))
    den = 1.0 + (0.3275911 * HALF_ROOT) * jnp.abs(x)
    t = pl.reciprocal(den, approx=True)
    t = t * (2.0 - den * t)
    poly = 0.5 * 1.061405429 * t - 0.5 * 1.453152027
    poly = poly * t + 0.5 * 1.421413741
    poly = poly * t - 0.5 * 0.284496736
    poly = poly * t + 0.5 * 0.254829592
    tail = poly * t * bell
    return jnp.where(x >= 0.0, 1.0 - tail, tail), bell


def dot_f32(a, b):
    return jnp.dot(a, b, precision=HIGHEST, preferred_element_type=jnp.float32)


def dot_bf16(a, b):
    return jnp.dot(a, b, preferred_element_type=jnp.float32)


def column(row):
    eye = lax.broadcasted_iota(jnp.int32, (64, 64), 0) == lax.broadcasted_iota(
        jnp.int32, (64, 64), 1
    )
    col = jnp.sum(jnp.where(eye, row, 0.0), axis=1, keepdims=True)
    return jnp.broadcast_to(col, (64, 256))


def step_kernel(
    state, damping, mask, gain, weight, pick, regrid, table_x, own_h, near_h, spec_h, fwd_h, inv_h,
    new_state, coef_all, grad_all,
    own, near, spec, fwd, inv,
    q, sec, faces, halo, edge, sink, a, b, gcol, wcol, g, pre, slope,
    fwd_sum, sib_sum, parts, inbox, total, mixed, ax, ax_hi, ax_lo,
    load_sem, halo_s, halo_r, sib_s, sib_r, part_s, part_r, mix_s, mix_r, hop_s, hop_r, z_s, z_r,
):
    grp, gx, gy = lax.axis_index("grp"), lax.axis_index("gx"), lax.axis_index("gy")
    chip, core = lax.div(gx, 2), lax.rem(gx, 2)
    cx, cy = lax.div(chip, 4), lax.rem(chip, 4)
    zme = grp * 2 + gy
    sibling = gx + 1 - 2 * core

    def chip_at(k, sign):
        dx, dy = lax.div(k, 4), lax.rem(k, 4)
        return lax.rem(cx + sign * dx + 4, 4) * 4 + lax.rem(cy + sign * dy + 4, 4)

    def z_at(k):
        zt = lax.rem(zme + k, ZPEERS)
        return {"grp": lax.div(zt, 2), "gy": lax.rem(zt, 2)}

    def each(lo, hi, f, unroll=1):
        def step(k, carry):
            f(k)
            return carry
        lax.fori_loop(lo, hi, step, 0, unroll=unroll)

    loads = [
        pltpu.make_async_copy(src, dst, load_sem.at[i])
        for i, (src, dst) in enumerate(
            ((fwd_h, fwd), (own_h, own), (near_h, near), (spec_h, spec), (inv_h, inv))
        )
    ]
    for c in loads:
        c.start()

    barrier = pltpu.get_barrier_semaphore()

    def greet(target):
        pl.semaphore_signal(barrier, inc=1, device_id=target, device_id_type=MESH)

    each(1, CHIPS, lambda k: greet({"gx": 2 * chip_at(k, 1) + core}))
    greet({"gx": sibling})
    greet({"gx": lax.rem(gx + 2 * core + 31, 32)})
    each(1, ZPEERS, lambda k: greet(z_at(k)))

    q[0:500, 0:128] = state[pl.ds(0, 500, stride=2), :]
    q[0:500, 128:256] = state[pl.ds(1, 500, stride=2), :]
    q[500:512, :] = jnp.zeros((12, 256), jnp.float32)
    a[...] = dot_f32(regrid[...], q[0:128, :]).astype(jnp.bfloat16).astype(jnp.float32)
    faces[0] = dot_f32(pick[...], q[...])
    gcol[...] = column(gain[...])
    wcol[...] = column(weight[...])
    sink[...] = mask[...].astype(jnp.float32) * damping[...]
    fwd_sum[...] = jnp.zeros_like(fwd_sum)

    pl.semaphore_wait(barrier, CHIPS - 1 + 2 + ZPEERS - 1)

    def halo_copy(stage, side):
        to = lax.rem(gx + (1, 31)[side], 32)
        return pltpu.make_async_remote_copy(
            src_ref=faces.at[stage, pl.ds(32 * side, 32)],
            dst_ref=halo.at[stage, side],
            send_sem=halo_s.at[stage, side],
            recv_sem=halo_r.at[stage, side],
            device_id={"gx": to},
            device_id_type=MESH,
        )

    for side in range(2):
        halo_copy(0, side).start()

    loads[0].wait()

    def transform(phase, j, slot):
        both = dot_bf16(g[slot], fwd[j])
        fwd_sum[phase, 0] += both[:, 0:128]
        fwd_sum[phase, 1] += both[:, 128:256]

    def lift(j, slot):
        for m in range(4):
            row = a[pl.ds(m * 16 + j, 1), :]
            for r in range(2):
                rows = pl.ds(32 * r, 32)
                x = gcol[rows, :] * row
                cdf, unused = normal_parts(x)
                g[slot, pl.ds(64 * m + 32 * r, 32), :] = (x * cdf).astype(jnp.bfloat16)
        transform(0, j, slot)

    def lift_pair(i):
        lift(2 * i, 0)
        lift(2 * i + 1, 1)

    each(0, 8, lift_pair)

    def sib_copy(phase):
        return pltpu.make_async_remote_copy(
            src_ref=fwd_sum.at[phase, 1 - core],
            dst_ref=sib_sum.at[phase],
            send_sem=sib_s.at[phase],
            recv_sem=sib_r.at[phase],
            device_id={"gx": sibling},
            device_id_type=MESH,
        )

    def part_copy(phase, k):
        return pltpu.make_async_remote_copy(
            src_ref=parts.at[phase, k],
            dst_ref=inbox.at[phase, k],
            send_sem=part_s.at[phase, k],
            recv_sem=part_r.at[phase, k],
            device_id={"gx": 2 * chip_at(k, 1) + core},
            device_id_type=MESH,
        )

    def expand(phase, k):
        base = chip_at(k, 1) * 128 + 8 * chip
        acc = jnp.zeros((64, 128), jnp.float32)
        for m in range(4):
            rows = pl.ds(64 * m, 64)
            acc = acc + table_x[base + 4 * core + m] * fwd_sum[phase, core, rows, :]
            acc = acc + table_x[base + 4 - 4 * core + m] * sib_sum[phase, rows, :]
        return acc

    def scatter(phase):
        sib_copy(phase).start()
        sib_copy(phase).wait()

        def send(k):
            parts[phase, k] = expand(phase, k)
            part_copy(phase, k).start()

        each(1, CHIPS, send)
        total[phase] = expand(phase, 0)

    def gather_sum(phase):
        def add(k, acc):
            part_copy(phase, k).wait_recv()
            return acc + inbox[phase, k]

        return lax.fori_loop(1, CHIPS, add, total[phase])

    def z_copy(phase, k):
        ref = (coef_all, grad_all)[phase]
        return pltpu.make_async_remote_copy(
            src_ref=ref.at[zme],
            dst_ref=ref.at[zme],
            send_sem=z_s.at[phase, k],
            recv_sem=z_r.at[phase, k],
            device_id=z_at(k),
            device_id_type=MESH,
        )

    lanes = lax.broadcasted_iota(jnp.int32, (32, 256), 1)
    ez = lax.rem(lanes, 16)

    def rates(stage, fields):
        for side in range(2):
            halo_copy(stage, side).wait_recv()
        ends = (gx == 0, gx == 31)
        for side in range(2):
            edge[pl.ds(32 * side, 32), :] = jnp.where(ends[side], 0.0, halo[stage, side])
        low, high = faces[stage, 64:96, :], faces[stage, 96:128, :]
        edge[64:96, :] = jnp.where(lanes < 16, 0.0, pltpu.roll(low, 16, 1))
        edge[96:128, :] = jnp.where(lanes >= 240, 0.0, pltpu.roll(high, 240, 1))
        low, high = faces[stage, 128:160, :], faces[stage, 160:192, :]
        edge[128:160, :] = jnp.where(ez == 0, 0.0, pltpu.roll(low, 1, 1))
        edge[160:192, :] = jnp.where(ez == 15, 0.0, pltpu.roll(high, 255, 1))
        rate = dot_f32(own[...], fields[...]) + dot_f32(near[...], edge[...])
        return rate - sink[...] * fields[...]

    scatter(0)

    loads[1].wait()
    loads[2].wait()
    sec[...] = q[...] + TIME_STEP * rates(0, q)
    faces[1] = dot_f32(pick[...], sec[...])
    for side in range(2):
        halo_copy(1, side).start()

    coef_all[pl.ds(zme, 1)] = gather_sum(0)[None]
    each(1, ZPEERS, lambda k: z_copy(0, k).start())

    loads[3].wait()

    def mix(i, acc):
        for u in range(8):
            c = i * 8 + u
            row = coef_all[pl.ds(zme, 1), pl.ds(c, 1), :].reshape(1, 128)
            acc = acc + spec[c] * row
        return acc

    mixed[0, 0] = lax.fori_loop(0, 8, mix, jnp.zeros((64, 128), jnp.float32)).astype(jnp.bfloat16)

    def mix_copy(k):
        return pltpu.make_async_remote_copy(
            src_ref=mixed.at[0, 0],
            dst_ref=mixed.at[0, k],
            send_sem=mix_s.at[k],
            recv_sem=mix_r.at[k],
            device_id={"gx": 2 * chip_at(k, 1) + core},
            device_id_type=MESH,
        )

    def hop_copy(k):
        return pltpu.make_async_remote_copy(
            src_ref=mixed.at[0, k],
            dst_ref=mixed.at[1, k],
            send_sem=hop_s.at[k],
            recv_sem=hop_r.at[k],
            device_id={"gx": sibling},
            device_id_type=MESH,
        )

    each(1, CHIPS, lambda k: mix_copy(k).start())
    hop_copy(0).start()

    done = 0.5 * (q[...] + sec[...] + TIME_STEP * rates(1, sec))
    new_state[pl.ds(0, 500, stride=2), :] = done[0:500, 0:128]
    new_state[pl.ds(1, 500, stride=2), :] = done[0:500, 128:256]
    b[...] = dot_f32(regrid[...], done[0:128, :]).astype(jnp.bfloat16).astype(jnp.float32)

    def add_modes(half, k, acc):
        base = chip_at(k, -1) * 128 + 4 * gx
        value = mixed[half, k].astype(jnp.float32)
        return tuple(acc[m] + table_x[base + m] * value for m in range(4))

    def own_half(k, acc):
        mix_copy(k).wait_recv()
        hop_copy(k).start()
        return add_modes(0, k, acc)

    def other_half(k, acc):
        hop_copy(k).wait_recv()
        return add_modes(1, k, acc)

    zeros = tuple(jnp.zeros((64, 128), jnp.float32) for unused in range(4))
    sums = lax.fori_loop(1, CHIPS, own_half, add_modes(0, 0, zeros))
    for m in range(4):
        ax[pl.ds(core, 1), pl.ds(64 * m, 64), :] = sums[m][None]
    sums = lax.fori_loop(0, CHIPS, other_half, zeros)
    for m in range(4):
        ax[pl.ds(1 - core, 1), pl.ds(64 * m, 64), :] = sums[m][None]
    for half in range(2):
        value = ax[half]
        high = value.astype(jnp.bfloat16)
        ax_hi[:, 128 * half : 128 * half + 128] = high
        ax_lo[:, 128 * half : 128 * half + 128] = (value - high.astype(jnp.float32)).astype(
            jnp.bfloat16
        )

    loads[4].wait()

    def back(j, slot):
        pre[slot] = dot_bf16(ax_hi[...], inv[j]) + dot_bf16(ax_lo[...], inv[j])
        for m in range(4):
            acc = jnp.zeros((8, 256), jnp.float32)
            for r in range(2):
                rows = pl.ds(64 * m + 32 * r, 32)
                x = pre[slot, rows, :]
                cdf, bell = normal_parts(x)
                slope[slot, rows, :] = cdf + x * bell * GAUSS_NORM
                act = x * cdf * wcol[pl.ds(32 * r, 32), :]
                acc = acc + jnp.sum(act.reshape(4, 8, 256), axis=0)
            misfit = jnp.sum(acc, axis=0, keepdims=True) - b[pl.ds(m * 16 + j, 1), :]
            misfit = (2.0 * LOSS_SCALE) * misfit
            for r in range(2):
                rows = pl.ds(64 * m + 32 * r, 32)
                value = misfit * wcol[pl.ds(32 * r, 32), :] * slope[slot, rows, :]
                g[slot, rows, :] = value.astype(jnp.bfloat16)
        transform(1, j, slot)

    def back_pair(i):
        back(2 * i, 0)
        back(2 * i + 1, 1)

    each(0, 8, back_pair)

    scatter(1)
    grad_all[pl.ds(zme, 1)] = gather_sum(1)[None]
    each(1, ZPEERS, lambda k: z_copy(1, k).start())

    def drain_chip(k):
        part_copy(0, k).wait_send()
        part_copy(1, k).wait_send()
        mix_copy(k).wait_send()

    each(1, CHIPS, drain_chip)
    each(0, CHIPS, lambda k: hop_copy(k).wait_send())
    for stage in range(2):
        for side in range(2):
            halo_copy(stage, side).wait_send()

    def drain_z(k):
        z_copy(0, k).wait()
        z_copy(1, k).wait()

    each(1, ZPEERS, drain_z)


def adam_kernel(coef, grad, spec, one, two, new_spec, new_one, new_two):
    block = spec.shape[0]
    first = pl.program_id(0) * block
    for c in range(block):
        acc = coef[0, pl.ds(first + c, 1), :] * grad[0]
        for t in range(1, ZPEERS):
            acc = acc + coef[t, pl.ds(first + c, 1), :] * grad[t]
        m1 = BETA_ONE * one[c].astype(jnp.float32) + (1.0 - BETA_ONE) * acc
        m2 = BETA_TWO * two[c].astype(jnp.float32) + (1.0 - BETA_TWO) * acc * acc
        den = jnp.sqrt(m2 * (1.0 / BIAS_TWO)) + EPSILON
        new_spec[c] = spec[c] - (LEARN_RATE / BIAS_ONE) * m1 / den
        new_one[c] = m1.astype(jnp.bfloat16)
        new_two[c] = m2.astype(jnp.bfloat16)


def per_device(state, damping, mask, gain, weight, spectral, moment_one, moment_two):
    own, near, pick, regrid, forward, inverse, along_x = tables()
    f32, bf16 = jnp.float32, jnp.bfloat16
    vmem = pl.BlockSpec(memory_space=pltpu.VMEM)
    smem = pl.BlockSpec(memory_space=pltpu.SMEM)
    anywhere = pl.BlockSpec(memory_space=pl.ANY)
    spec_t = jnp.transpose(spectral, (1, 2, 0))
    dma = pltpu.SemaphoreType.DMA
    new_state, coef_all, grad_all = pl.pallas_call(
        step_kernel,
        out_shape=(
            jax.ShapeDtypeStruct((1000, 128), f32),
            jax.ShapeDtypeStruct((ZPEERS, 64, 128), f32),
            jax.ShapeDtypeStruct((ZPEERS, 64, 128), f32),
        ),
        in_specs=[vmem] * 7 + [smem] + [anywhere] * 5,
        out_specs=(vmem, vmem, vmem),
        scratch_shapes=[
            pltpu.VMEM((512, 512), f32),
            pltpu.VMEM((512, 192), f32),
            pltpu.VMEM((64, 64, 128), f32),
            pltpu.VMEM((16, 256, 256), bf16),
            pltpu.VMEM((16, 256, 256), bf16),
            pltpu.VMEM((512, 256), f32),
            pltpu.VMEM((512, 256), f32),
            pltpu.VMEM((2, 192, 256), f32),
            pltpu.VMEM((2, 2, 32, 256), f32),
            pltpu.VMEM((192, 256), f32),
            pltpu.VMEM((1, 256), f32),
            pltpu.VMEM((64, 256), f32),
            pltpu.VMEM((64, 256), f32),
            pltpu.VMEM((64, 256), f32),
            pltpu.VMEM((64, 256), f32),
            pltpu.VMEM((2, 256, 256), bf16),
            pltpu.VMEM((2, 256, 256), f32),
            pltpu.VMEM((2, 256, 256), f32),
            pltpu.VMEM((2, 2, 256, 128), f32),
            pltpu.VMEM((2, 256, 128), f32),
            pltpu.VMEM((2, CHIPS, 64, 128), f32),
            pltpu.VMEM((2, CHIPS, 64, 128), f32),
            pltpu.VMEM((2, 64, 128), f32),
            pltpu.VMEM((2, CHIPS, 64, 128), bf16),
            pltpu.VMEM((2, 256, 128), f32),
            pltpu.VMEM((256, 256), bf16),
            pltpu.VMEM((256, 256), bf16),
            dma((5,)),
            dma((2, 2)),
            dma((2, 2)),
            dma((2,)),
            dma((2,)),
            dma((2, CHIPS)),
            dma((2, CHIPS)),
            dma((CHIPS,)),
            dma((CHIPS,)),
            dma((CHIPS,)),
            dma((CHIPS,)),
            dma((2, ZPEERS)),
            dma((2, ZPEERS)),
        ],
        compiler_params=pltpu.CompilerParams(
            collective_id=0, has_side_effects=True, vmem_limit_bytes=40 * 1024 * 1024
        ),
        name="step",
    )(
        state.reshape(1000, 128), damping, mask, gain.reshape(1, 64), weight.reshape(1, 64),
        pick, regrid, along_x, own, near, spec_t, forward, inverse,
    )
    block = 8
    whole = pl.BlockSpec((ZPEERS, 64, 128), lambda i: (0, 0, 0))
    tile = pl.BlockSpec((block, 64, 128), lambda i: (i, 0, 0))
    new_spec, new_one, new_two = pl.pallas_call(
        adam_kernel,
        grid=(64 // block,),
        out_shape=(
            jax.ShapeDtypeStruct((64, 64, 128), f32),
            jax.ShapeDtypeStruct((64, 64, 128), bf16),
            jax.ShapeDtypeStruct((64, 64, 128), bf16),
        ),
        in_specs=[whole, whole, tile, tile, tile],
        out_specs=(tile, tile, tile),
        compiler_params=pltpu.CompilerParams(vmem_limit_bytes=16 * 1024 * 1024),
        name="update",
    )(
        coef_all, grad_all, spec_t,
        jnp.transpose(moment_one, (1, 2, 0)), jnp.transpose(moment_two, (1, 2, 0)),
    )
    back = (2, 0, 1)
    return (
        new_state.reshape(state.shape),
        jnp.transpose(new_spec, back),
        jnp.transpose(new_one, back),
        jnp.transpose(new_two, back),
    )


def solution(mesh):
    in_specs = (
        P(("grp", "gy"), None, None, "gx", None),
        P("gx", None),
        P("gx", None),
        P(),
        P(),
        P("gx", None, None),
        P("gx", None, None),
        P("gx", None, None),
    )
    out_specs = (
        P(("grp", "gy"), None, None, "gx", None),
        P("gx", None, None),
        P("gx", None, None),
        P("gx", None, None),
    )
    return jax.shard_map(
        per_device, mesh=mesh, in_specs=in_specs, out_specs=out_specs, check_vma=False
    )
```

profile of v0, /device:TPU:1, one launch (start us, length us, event | category | flops | bytes accessed | tf_op | source)
XLA Modules:
  0.0 80.7 jit_solution(12881941500936831549)
XLA Ops:
  0.6 0.0 copy-start
  0.6 1.6 %copy-done = f32[128,64,64]{0,2,1:T(8,128)S(1)} copy-done((f32[128,64,64]{0,2,1:T(8,128)S(1)}, f32[128,64,64]{0,2,1:T(8,128)}, u32[]{:S(2)}) %copy-start) | copy-done | bytes 2097176
  2.2 0.0 copy-start.1
  2.2 1.6 %copy-done.1 = bf16[16,256,256]{2,1,0:T(8,128)(2,1)S(1)} copy-done((bf16[16,256,256]{2,1,0:T(8,128)(2,1)S(1)}, bf16[16,256,256]{2,1,0:T(8,128)(2,1)}, u32[]{:S(2)}) %copy-start.1) | copy-done | bytes 2097176
  3.8 0.0 copy-start.2
  3.8 1.6 %copy-done.2 = bf16[16,256,256]{2,1,0:T(8,128)(2,1)S(1)} copy-done((bf16[16,256,256]{2,1,0:T(8,128)(2,1)S(1)}, bf16[16,256,256]{2,1,0:T(8,128)(2,1)}, u32[]{:S(2)}) %copy-start.2) | copy-done | bytes 2097176
  5.4 0.0 copy-start.5
  5.4 1.2 %copy-done.5 = f32[512,512]{1,0:T(8,128)S(1)} copy-done((f32[512,512]{1,0:T(8,128)S(1)}, f32[512,512]{1,0:T(8,128)}, u32[]{:S(2)}) %copy-start.5) | copy-done | bytes 1048600
  6.6 0.0 copy-start.6
  6.6 1.0 %copy-done.6 = f32[512,192]{1,0:T(8,128)S(1)} copy-done((f32[512,192]{1,0:T(8,128)S(1)}, f32[512,192]{1,0:T(8,128)}, u32[]{:S(2)}) %copy-start.6) | copy-done | bytes 393240
  7.7 0.0 copy-start.7
  7.7 1.0 %copy-done.7 = f32[1,4,125,1,256]{4,3,2,1,0:T(1,128)S(1)} copy-done((f32[1,4,125,1,256]{4,3,2,1,0:T(1,128)S(1)}, f32[1,4,125,1,256]{4,3,2,1,0:T(1,128)}, u32[]{:S(2)}) %copy-start.7) | copy-done | bytes 512024
  8.7 1.0 %copy-done.8 = f32[192,512]{1,0:T(8,128)S(1)} copy-done((f32[192,512]{1,0:T(8,128)S(1)}, f32[192,512]{1,0:T(8,128)}, u32[]{:S(2)}) %copy-start.8) | copy-done | bytes 393240
  9.7 0.8 copy-done.9
  10.5 0.7 copy-done.10
  11.2 0.7 copy-done.11
  11.8 0.7 copy-done.12
  12.5 0.7 copy-done.13
  13.2 0.7 copy-done.14
  13.8 61.2 %step.1 = (f32[1000,128]{1,0:T(8,128)S(1)}, f32[8,64,128]{2,1,0:T(8,128)S(1)}, f32[8,64,128]{2,1,0:T(8,128)S(1)}) custom-call(f32[1000,128]{1,0:T(8,128)S(1)} %bitcast.14, f32[1,256]{1,0:T(1,128)S(1)} %copy-done.11, s32[1,256]{1,0:T(1,128)S(1)} %copy-done.12, f32[1,64]{1,0:T(1,128)S(1)} %bitcast.16, f32[1,64]{1,0:T(1,128)S(1)} %bitcast.17, ...), custom_call_target="tpu_custom_call" | custom-call | tf_op jit(solution)/shard_map/step/pallas_call | solution.py:483
  75.0 0.0 copy-done.3
  75.0 0.0 copy-done.4
  75.1 4.9 %update.1 = (f32[64,64,128]{2,1,0:T(8,128)}, bf16[64,64,128]{2,1,0:T(8,128)(2,1)}, bf16[64,64,128]{2,1,0:T(8,128)(2,1)}) custom-call(f32[8,64,128]{2,1,0:T(8,128)S(1)} %get-tuple-element.11.coef, f32[8,64,128]{2,1,0:T(8,128)S(1)} %get-tuple-element.12.grad, f32[64,64,128]{2,1,0:T(8,128)S(1)} %bitcast.11, bf16[64,64,128]{2,1,0:T(8,128)(2,1)S(1)} %bitcast.12, ...), custom_call_target="tpu_custom_call" | custom-call | tf_op jit(solution)/shard_map/update/pallas_call | solution.py:545
  79.9 0.8 copy.22
  (9 shorter events, 0.0 us)
Async XLA Ops:
  0.6 1.6 %copy-start = (f32[128,64,64]{0,2,1:T(8,128)S(1)}, f32[128,64,64]{0,2,1:T(8,128)}, u32[]{:S(2)}) copy-start(f32[128,64,64]{0,2,1:T(8,128)} %param.20) | copy-start | bytes 6291460
  2.2 1.6 %copy-start.1 = (bf16[16,256,256]{2,1,0:T(8,128)(2,1)S(1)}, bf16[16,256,256]{2,1,0:T(8,128)(2,1)}, u32[]{:S(2)}) copy-start(bf16[16,256,256]{2,1,0:T(8,128)(2,1)} %constant.28.inv_h) | copy-start | bytes 6291460
  3.8 1.6 %copy-start.2 = (bf16[16,256,256]{2,1,0:T(8,128)(2,1)S(1)}, bf16[16,256,256]{2,1,0:T(8,128)(2,1)}, u32[]{:S(2)}) copy-start(bf16[16,256,256]{2,1,0:T(8,128)(2,1)} %constant.27.fwd_h) | copy-start | bytes 6291460
  5.4 1.2 %copy-start.5 = (f32[512,512]{1,0:T(8,128)S(1)}, f32[512,512]{1,0:T(8,128)}, u32[]{:S(2)}) copy-start(f32[512,512]{1,0:T(8,128)} %constant.19.clone.own_h) | copy-start | bytes 3145732
  6.6 1.0 %copy-start.6 = (f32[512,192]{1,0:T(8,128)S(1)}, f32[512,192]{1,0:T(8,128)}, u32[]{:S(2)}) copy-start(f32[512,192]{1,0:T(8,128)} %constant.20.clone.near_h) | copy-start | bytes 1179652
  7.7 1.0 %copy-start.7 = (f32[1,4,125,1,256]{4,3,2,1,0:T(1,128)S(1)}, f32[1,4,125,1,256]{4,3,2,1,0:T(1,128)}, u32[]{:S(2)}) copy-start(f32[1,4,125,1,256]{4,3,2,1,0:T(1,128)} %param.15) | copy-start | bytes 1536004
  8.7 1.0 %copy-start.8 = (f32[192,512]{1,0:T(8,128)S(1)}, f32[192,512]{1,0:T(8,128)}, u32[]{:S(2)}) copy-start(f32[192,512]{1,0:T(8,128)} %constant.17.clone.pick) | copy-start | bytes 1179652
  9.7 0.8 copy-start.9
  10.5 0.7 copy-start.10
  11.2 0.7 copy-start.11
  11.8 0.7 copy-start.12
  12.5 0.7 copy-start.13
  13.2 0.7 copy-start.14
  13.8 61.2 %copy-start.3 = (bf16[128,64,64]{0,2,1:T(8,128)(2,1)S(1)}, bf16[128,64,64]{0,2,1:T(8,128)(2,1)}, u32[]{:S(2)}) copy-start(bf16[128,64,64]{0,2,1:T(8,128)(2,1)} %param.21) | copy-start | bytes 3145732
  13.8 61.2 %copy-start.4 = (bf16[128,64,64]{0,2,1:T(8,128)(2,1)S(1)}, bf16[128,64,64]{0,2,1:T(8,128)(2,1)}, u32[]{:S(2)}) copy-start(bf16[128,64,64]{0,2,1:T(8,128)(2,1)} %param.22) | copy-start | bytes 3145732
where the time goes:
time: 81.6 us; the launch traced here: 80.7 us
  Pallas kernels  66.1 us (81%)
  local copies, waits for them, and re-layouts  14 us (17%)
    pallas_call x1, Pallas kernels, per_device(): pl.pallas_call(step_kernel, out_shape=(jax.ShapeDtypeStruct((1000, 128),...  61.2 us
    unnamed x31, local copies, waits for them, and re-layouts  14 us
    pallas_call x1, Pallas kernels, per_device(): pl.pallas_call(adam_kernel, grid=(64 // block,), out_shape=(jax.ShapeDtyp...  4.88 us

commit v1 on v0

v1 whole, which is shorter than its diff:
```python
import math

import jax
import jax.numpy as jnp
import numpy as np
from jax import lax
from jax.experimental import pallas as pl
from jax.experimental.pallas import tpu as pltpu
from jax.sharding import PartitionSpec as P

MESH = pl.DeviceIdType.MESH
HIGHEST = lax.Precision.HIGHEST
KM = 16
CHIPS = 16
ZPEERS = 8
TIME_STEP = 0.02
FACE_GAIN = 10.0
LOSS_SCALE = 1.0 / 2048.0
LEARN_RATE = 0.001
BETA_ONE = 0.9
BETA_TWO = 0.999
BIAS_ONE = 1.0 - BETA_ONE**10
BIAS_TWO = 1.0 - BETA_TWO**10
EPSILON = 1e-08
HALF_ROOT = 1.0 / math.sqrt(2.0)
GAUSS_NORM = 1.0 / math.sqrt(2.0 * math.pi)
LOG2E = 1.4426950408889634


def lagrange(nodes, column, point):
    value = 1.0
    for other in range(len(nodes)):
        if other != column:
            value = value * (point - nodes[other]) / (nodes[column] - nodes[other])
    return value


def lagrange_slope(nodes, column, point):
    total = 0.0
    for skipped in range(len(nodes)):
        if skipped != column:
            factor = 1.0 / (nodes[column] - nodes[skipped])
            for other in range(len(nodes)):
                if other != column and other != skipped:
                    factor = factor * (point - nodes[other]) / (nodes[column] - nodes[other])
            total = total + factor
    return total


def gll_tables():
    nodes = [-1.0, -math.sqrt(3.0 / 7.0), 0.0, math.sqrt(3.0 / 7.0), 1.0]
    slopes = np.array([[lagrange_slope(nodes, c, nodes[r]) for c in range(5)] for r in range(5)])
    interp = np.array(
        [[lagrange(nodes, c, -1.0 + (2.0 * m + 1.0) / 4.0) for c in range(5)] for m in range(4)]
    )
    return slopes.astype(np.float32), interp.astype(np.float32)


def fourier_table(length, kept):
    angles = np.arange(length) * (2.0 * math.pi / length)
    rows = []
    for freq in range(kept // 2 + 1):
        factor = math.sqrt(1.0 / length) if freq == 0 else math.sqrt(2.0 / length)
        rows.append(factor * np.cos(freq * angles))
    for freq in range(1, kept // 2):
        rows.append(math.sqrt(2.0 / length) * np.sin(freq * angles))
    return np.stack(rows)


def node_of(index, axis, value):
    out = list(index)
    out[axis] = value
    return 25 * out[0] + 5 * out[1] + out[2]


def solver_tables(slopes):
    own = np.zeros((512, 512))
    near = np.zeros((512, 192))
    pick = np.zeros((192, 512))
    for i1 in range(5):
        for i2 in range(5):
            for i3 in range(5):
                index = (i1, i2, i3)
                node = 25 * i1 + 5 * i2 + i3
                for d in range(3):
                    u = 125 * (1 + d)
                    for k in range(5):
                        other = node_of(index, d, k)
                        own[node, u + other] += -2.0 * slopes[index[d], k]
                        own[u + node, other] += -2.0 * slopes[index[d], k]
                    rest = [index[e] for e in range(3) if e != d]
                    face = 5 * rest[0] + rest[1]
                    low, high = 64 * d + face, 64 * d + 32 + face
                    if index[d] == 0:
                        own[node, u + node] -= FACE_GAIN
                        own[node, node] -= FACE_GAIN
                        own[u + node, u + node] -= FACE_GAIN
                        own[u + node, node] -= FACE_GAIN
                        near[node, low] = FACE_GAIN
                        near[u + node, low] = FACE_GAIN
                        pick[high, node] = 1.0
                        pick[high, u + node] = -1.0
                    if index[d] == 4:
                        own[node, u + node] += FACE_GAIN
                        own[node, node] -= FACE_GAIN
                        own[u + node, node] += FACE_GAIN
                        own[u + node, u + node] -= FACE_GAIN
                        near[node, high] = FACE_GAIN
                        near[u + node, high] = -FACE_GAIN
                        pick[low, node] = 1.0
                        pick[low, u + node] = 1.0
    return tuple(t.astype(np.float32) for t in (own, near, pick))


def tables():
    slopes, interp = gll_tables()
    own, near, pick = solver_tables(slopes.astype(np.float64))
    interp = interp.astype(np.float64)
    regrid = np.zeros((64, 128), np.float32)
    regrid[:, :125] = np.kron(np.kron(interp, interp), interp).astype(np.float32)
    joint = np.kron(fourier_table(64, KM), fourier_table(64, KM)).astype(np.float32)
    joint = joint.reshape(256, 16, 4, 16, 4).transpose(2, 4, 0, 1, 3).reshape(16, 256, 256)
    inverse = jnp.asarray(joint).astype(jnp.bfloat16)
    forward = jnp.asarray(joint.transpose(0, 2, 1).reshape(4096, 256)).astype(jnp.bfloat16)
    along_x = jnp.asarray(fourier_table(128, KM), dtype=jnp.float32).astype(jnp.bfloat16)
    along_x = along_x.astype(jnp.float32).reshape(-1)
    return own, near, pick, regrid, forward, inverse, along_x


def normal_tail(x):
    bell = jnp.exp2(x * x * (-0.5 * LOG2E))
    den = 1.0 + (0.3275911 * HALF_ROOT) * jnp.abs(x)
    t = pl.reciprocal(den, approx=True)
    t = t * (2.0 - den * t)
    poly = 0.5 * 1.061405429 * t - 0.5 * 1.453152027
    poly = poly * t + 0.5 * 1.421413741
    poly = poly * t - 0.5 * 0.284496736
    poly = poly * t + 0.5 * 0.254829592
    return poly * t * bell, bell


def dot_f32(a, b):
    return jnp.dot(a, b, precision=HIGHEST, preferred_element_type=jnp.float32)


def dot_bf16(a, b):
    return jnp.dot(a, b, preferred_element_type=jnp.float32)


def column(row):
    eye = lax.broadcasted_iota(jnp.int32, (64, 64), 0) == lax.broadcasted_iota(
        jnp.int32, (64, 64), 1
    )
    col = jnp.sum(jnp.where(eye, row, 0.0), axis=1, keepdims=True)
    return jnp.broadcast_to(col, (64, 256))


def step_kernel(
    state_h, damping_h, mask_h, gain_h, weight_h, pick_h, regrid_h, table_h, own_h, near_h, spec_h,
    fwd_h, inv_h,
    new_state, coef_all, grad_all,
    state, damping, mask, gain, weight, pick, regrid, table_x, own, near, spec, fwd, inv,
    q, sec, faces, halo, edge, sink, a, b, gcol, wcol, g_a, g_b, pre, slope,
    fwd_sum, sib_sum, parts, inbox, total, mixed,
    ax, ax_hi, ax_lo,
    load_sem, halo_s, halo_r, sib_s, sib_r, part_s, part_r, mix_s, mix_r, hop_s, hop_r, z_s, z_r,
):
    grp, gx, gy = lax.axis_index("grp"), lax.axis_index("gx"), lax.axis_index("gy")
    chip, core = lax.div(gx, 2), lax.rem(gx, 2)
    cx, cy = lax.div(chip, 4), lax.rem(chip, 4)
    zme = grp * 2 + gy
    sibling = gx + 1 - 2 * core

    along = [[lax.rem(c + step, 4) for step in range(4)] for c in (cx, cy)]

    def chip_at(k, sign):
        return along[0][sign * (k // 4) % 4] * 4 + along[1][sign * (k % 4) % 4]

    def z_at(k):
        zt = lax.rem(zme + k, ZPEERS)
        return {"grp": lax.div(zt, 2), "gy": lax.rem(zt, 2)}

    def hops(k):
        return min(k // 4, 4 - k // 4) + min(k % 4, 4 - k % 4)

    others = sorted(range(1, CHIPS), key=hops)
    far = others[::-1]
    z_far = (4, 3, 5, 2, 6, 1, 7)

    def each(lo, hi, f, unroll=1):
        def step(k, carry):
            f(k)
            return carry
        lax.fori_loop(lo, hi, step, 0, unroll=unroll)

    fwd_parts = [pl.ds(1024 * i, 1024) for i in range(4)]
    moves = [
        (state_h.at[pl.ds(0, 256)], state.at[pl.ds(0, 256)]),
        (regrid_h, regrid),
        (gain_h, gain),
        *((fwd_h.at[part], fwd.at[part]) for part in fwd_parts),
        (state_h.at[pl.ds(256, 744)], state.at[pl.ds(256, 744)]),
        (pick_h, pick),
        (table_h, table_x),
        (damping_h, damping),
        (mask_h, mask),
        (own_h, own),
        (near_h, near),
        (spec_h, spec),
        (weight_h, weight),
        (inv_h, inv),
    ]
    loads = [pltpu.make_async_copy(*m, load_sem.at[i]) for i, m in enumerate(moves)]
    for c in loads[:7]:
        c.start()

    barrier = pltpu.get_barrier_semaphore()

    def greet(target):
        pl.semaphore_signal(barrier, inc=1, device_id=target, device_id_type=MESH)

    for k in others:
        greet({"gx": 2 * chip_at(k, 1) + core})
    greet({"gx": sibling})
    greet({"gx": lax.rem(gx + 2 * core + 31, 32)})
    for k in z_far:
        greet(z_at(k))

    for c in loads[:3]:
        c.wait()
    for c in loads[7:]:
        c.start()
    q[0:128, 0:128] = state[pl.ds(0, 128, stride=2), :]
    q[0:128, 128:256] = state[pl.ds(1, 128, stride=2), :]
    a[...] = dot_f32(regrid[...], q[0:128, :]).astype(jnp.bfloat16).astype(jnp.float32)
    gcol[...] = column(gain[...])
    fwd_sum[...] = jnp.zeros_like(fwd_sum)
    g_b[...] = jnp.zeros_like(g_b)

    def halo_copy(stage, side):
        to = lax.rem(gx + (1, 31)[side], 32)
        return pltpu.make_async_remote_copy(
            src_ref=faces.at[stage, pl.ds(32 * side, 32)],
            dst_ref=halo.at[stage, side],
            send_sem=halo_s.at[stage, side],
            recv_sem=halo_r.at[stage, side],
            device_id={"gx": to},
            device_id_type=MESH,
        )

    def rows_of(m, r):
        return pl.ds(128 * r + 32 * m, 32)

    def sib_copy(phase, r):
        return pltpu.make_async_remote_copy(
            src_ref=fwd_sum.at[phase, 1 - core, r],
            dst_ref=sib_sum.at[phase, r],
            send_sem=sib_s.at[phase, r],
            recv_sem=sib_r.at[phase, r],
            device_id={"gx": sibling},
            device_id_type=MESH,
        )

    def part_copy(phase, r, k):
        return pltpu.make_async_remote_copy(
            src_ref=parts.at[phase, r, k],
            dst_ref=inbox.at[phase, r, k],
            send_sem=part_s.at[phase, r, k],
            recv_sem=part_r.at[phase, r, k],
            device_id={"gx": 2 * chip_at(k, 1) + core},
            device_id_type=MESH,
        )

    def expand(phase, r, k):
        base = chip_at(k, 1) * 128 + 8 * chip
        acc = jnp.zeros((32, 128), jnp.float32)
        for m in range(4):
            rows = pl.ds(32 * m, 32)
            acc = acc + table_x[base + 4 * core + m] * fwd_sum[phase, core, r, rows, :]
            acc = acc + table_x[base + 4 - 4 * core + m] * sib_sum[phase, r, rows, :]
        return acc

    def scatter(phase, r):
        sib_copy(phase, r).wait()
        for k in far:
            parts[phase, r, k] = expand(phase, r, k)
            part_copy(phase, r, k).start()
        total[phase, r] = expand(phase, r, 0)

    def gather_sum(phase, r):
        ref = (coef_all, grad_all)[phase]
        summed = total[phase, r]
        for k in others:
            part_copy(phase, r, k).wait_recv()
            summed = summed + inbox[phase, r, k]
        ref[pl.ds(zme, 1), pl.ds(32 * r, 32), :] = summed[None]

    def z_copy(phase, r, k):
        ref = (coef_all, grad_all)[phase].at[zme, pl.ds(32 * r, 32)]
        return pltpu.make_async_remote_copy(
            src_ref=ref,
            dst_ref=ref,
            send_sem=z_s.at[phase, r, k],
            recv_sem=z_r.at[phase, r, k],
            device_id=z_at(k),
            device_id_type=MESH,
        )

    def transform(phase, i, g, halves):
        points = pl.ds(pl.multiple_of(512 * i, 512), 512)
        both = dot_bf16(g[pl.ds(128 * halves[0], 128 * len(halves)), :], fwd[points, :])
        for n, r in enumerate(halves):
            rows = slice(128 * n, 128 * n + 128)
            fwd_sum[phase, 0, r] += both[rows, 0:128]
            fwd_sum[phase, 1, r] += both[rows, 128:256]

    def lift(j, g, side):
        for m in range(4):
            row = a[pl.ds(m * 16 + j, 1), :]
            for r in range(2):
                x = gcol[pl.ds(32 * r, 32), :] * row
                lifted = jnp.maximum(x, 0.0) - jnp.abs(x) * normal_tail(x)[0]
                g[rows_of(m, r), 256 * side : 256 * side + 256] = lifted.astype(jnp.bfloat16)

    for i in range(4):
        loads[3 + i].wait()

    def lift_four(i):
        lift(4 * i, g_a, 0)
        lift(4 * i + 1, g_a, 1)
        transform(0, lax.rem(2 * i + 7, 8), g_b, (0, 1))
        lift(4 * i + 2, g_b, 0)
        lift(4 * i + 3, g_b, 1)
        transform(0, 2 * i, g_a, (0, 1))

    each(0, 4, lift_four)
    transform(0, 7, g_b, (0, 1))

    pl.semaphore_wait(barrier, CHIPS - 1 + 2 + ZPEERS - 1)

    for r in range(2):
        sib_copy(0, r).start()
    lanes = lax.broadcasted_iota(jnp.int32, (32, 256), 1)
    ez = lax.rem(lanes, 16)

    def rates(stage, fields):
        for side in range(2):
            halo_copy(stage, side).wait_recv()
        ends = (gx == 0, gx == 31)
        for side in range(2):
            edge[pl.ds(32 * side, 32), :] = jnp.where(ends[side], 0.0, halo[stage, side])
        low, high = faces[stage, 64:96, :], faces[stage, 96:128, :]
        edge[64:96, :] = jnp.where(lanes < 16, 0.0, pltpu.roll(low, 16, 1))
        edge[96:128, :] = jnp.where(lanes >= 240, 0.0, pltpu.roll(high, 240, 1))
        low, high = faces[stage, 128:160, :], faces[stage, 160:192, :]
        edge[128:160, :] = jnp.where(ez == 0, 0.0, pltpu.roll(low, 1, 1))
        edge[160:192, :] = jnp.where(ez == 15, 0.0, pltpu.roll(high, 255, 1))
        rate = dot_f32(own[...], fields[...]) + dot_f32(near[...], edge[...])
        return rate - sink[...] * fields[...]

    for c in loads[7:14]:
        c.wait()
    q[128:500, 0:128] = state[pl.ds(256, 372, stride=2), :]
    q[128:500, 128:256] = state[pl.ds(257, 372, stride=2), :]
    q[500:512, :] = jnp.zeros((12, 256), jnp.float32)
    sink[...] = mask[...].astype(jnp.float32) * damping[...]
    faces[0] = dot_f32(pick[...], q[...])
    for side in range(2):
        halo_copy(0, side).start()
    for r in range(2):
        scatter(0, r)

    sec[...] = q[...] + TIME_STEP * rates(0, q)
    faces[1] = dot_f32(pick[...], sec[...])
    for side in range(2):
        halo_copy(1, side).start()

    for r in range(2):
        gather_sum(0, r)

    loads[14].wait()

    def mix(i, acc):
        for u in range(8):
            c = i * 8 + u
            row = coef_all[pl.ds(zme, 1), pl.ds(c, 1), :].reshape(1, 128)
            acc = acc + spec[c] * row
        return acc

    mixed[0, 0] = lax.fori_loop(0, 8, mix, jnp.zeros((64, 128), jnp.float32)).astype(jnp.bfloat16)

    def mix_copy(k):
        return pltpu.make_async_remote_copy(
            src_ref=mixed.at[0, 0],
            dst_ref=mixed.at[0, k],
            send_sem=mix_s.at[k],
            recv_sem=mix_r.at[k],
            device_id={"gx": 2 * chip_at(k, 1) + core},
            device_id_type=MESH,
        )

    def hop_copy(k):
        direct = hops(k) > 2
        return pltpu.make_async_remote_copy(
            src_ref=mixed.at[0, 0 if direct else k],
            dst_ref=mixed.at[1, k],
            send_sem=hop_s.at[k],
            recv_sem=hop_r.at[k],
            device_id={"gx": 2 * chip_at(k, 1) + 1 - core if direct else sibling},
            device_id_type=MESH,
        )

    for k in far:
        mix_copy(k).start()
        if hops(k) > 2:
            hop_copy(k).start()
    hop_copy(0).start()
    for r in range(2):
        for k in z_far:
            z_copy(0, r, k).start()

    done = 0.5 * (q[...] + sec[...] + TIME_STEP * rates(1, sec))
    new_state[pl.ds(0, 500, stride=2), :] = done[0:500, 0:128]
    new_state[pl.ds(1, 500, stride=2), :] = done[0:500, 128:256]
    b[...] = dot_f32(regrid[...], done[0:128, :]).astype(jnp.bfloat16).astype(jnp.float32)

    def add_modes(half, k, acc):
        base = chip_at(k, -1) * 128 + 4 * gx
        value = mixed[half, k].astype(jnp.float32)
        return tuple(acc[m] + table_x[base + m] * value for m in range(4))

    zeros = tuple(jnp.zeros((64, 128), jnp.float32) for unused in range(4))
    sums = add_modes(0, 0, zeros)
    for k in others:
        mix_copy(k).wait_recv()
        if hops(k) <= 2:
            hop_copy(k).start()
        sums = add_modes(0, k, sums)
    for m in range(4):
        for r in range(2):
            ax[pl.ds(core, 1), rows_of(m, r), :] = sums[m][None, 32 * r : 32 * r + 32]
    sums = zeros
    for k in (0, *others):
        hop_copy(k).wait_recv()
        sums = add_modes(1, k, sums)
    for m in range(4):
        for r in range(2):
            ax[pl.ds(1 - core, 1), rows_of(m, r), :] = sums[m][None, 32 * r : 32 * r + 32]
    for half in range(2):
        value = ax[half]
        high = value.astype(jnp.bfloat16)
        ax_hi[:, 128 * half : 128 * half + 128] = high
        ax_lo[:, 128 * half : 128 * half + 128] = (value - high.astype(jnp.float32)).astype(
            jnp.bfloat16
        )

    loads[15].wait()
    loads[16].wait()
    wcol[...] = column(weight[...])
    g_b[...] = jnp.zeros_like(g_b)

    def inverse(j, slot):
        pre[slot] = dot_bf16(ax_hi[...], inv[j]) + dot_bf16(ax_lo[...], inv[j])

    def back(j, slot, g, side):
        cols = slice(256 * side, 256 * side + 256)
        for m in range(4):
            acc = jnp.zeros((8, 256), jnp.float32)
            for r in range(2):
                rows = rows_of(m, r)
                x = pre[slot, rows, :]
                tail, bell = normal_tail(x)
                cdf = jnp.where(x >= 0.0, 1.0 - tail, tail)
                slope[slot, rows, :] = cdf + x * bell * GAUSS_NORM
                act = x * cdf * wcol[pl.ds(32 * r, 32), :]
                acc = acc + jnp.sum(act.reshape(4, 8, 256), axis=0)
            misfit = jnp.sum(acc, axis=0, keepdims=True) - b[pl.ds(m * 16 + j, 1), :]
            misfit = (2.0 * LOSS_SCALE) * misfit
            for r in range(2):
                rows = rows_of(m, r)
                value = misfit * wcol[pl.ds(32 * r, 32), :] * slope[slot, rows, :]
                g[rows, cols] = value.astype(jnp.bfloat16)

    def back_four(i):
        inverse(4 * i + 1, 1)
        back(4 * i, 0, g_a, 0)
        inverse(4 * i + 2, 0)
        back(4 * i + 1, 1, g_a, 1)
        transform(1, lax.rem(2 * i + 7, 8), g_b, (0, 1))
        inverse(4 * i + 3, 1)
        back(4 * i + 2, 0, g_b, 0)
        inverse(lax.rem(4 * i + 4, 16), 0)
        back(4 * i + 3, 1, g_b, 1)
        transform(1, 2 * i, g_a, (0, 1))

    inverse(0, 0)
    each(0, 4, back_four)
    transform(1, 7, g_b, (0, 1))

    for r in range(2):
        sib_copy(1, r).start()
    for r in range(2):
        scatter(1, r)
    for r in range(2):
        gather_sum(1, r)
        for k in z_far:
            z_copy(1, r, k).start()

    for k in others:
        for phase in range(2):
            for r in range(2):
                part_copy(phase, r, k).wait_send()
        mix_copy(k).wait_send()
    for k in range(CHIPS):
        hop_copy(k).wait_send()
    for stage in range(2):
        for side in range(2):
            halo_copy(stage, side).wait_send()
    for phase in range(2):
        for r in range(2):
            for k in z_far:
                z_copy(phase, r, k).wait()


def update_kernel(
    coef, grad, spec, one, two, state, new_spec, new_one, new_two, new_state,
    out_spec, out_one, out_two, sem,
):
    move = pltpu.make_async_copy(state, new_state, sem.at[0, 3])
    move.start()
    block = 8

    def chunk(i):
        rows = pl.ds(block * i, block)
        return [
            pltpu.make_async_copy(src.at[rows], dst.at[rows], sem.at[i, n])
            for n, (src, dst) in enumerate(
                ((out_spec, new_spec), (out_one, new_one), (out_two, new_two))
            )
        ]

    def run(i, carry):
        for n in range(block):
            c = block * i + n
            acc = coef[0, pl.ds(c, 1), :] * grad[0]
            for t in range(1, ZPEERS):
                acc = acc + coef[t, pl.ds(c, 1), :] * grad[t]
            m1 = BETA_ONE * one[c].astype(jnp.float32) + (1.0 - BETA_ONE) * acc
            m2 = BETA_TWO * two[c].astype(jnp.float32) + (1.0 - BETA_TWO) * acc * acc
            scaled = m2 * (1.0 / BIAS_TWO)
            den = scaled * lax.rsqrt(scaled) + EPSILON
            inverse = pl.reciprocal(den, approx=True)
            inverse = inverse * (2.0 - den * inverse)
            out_spec[c] = spec[c] - (LEARN_RATE / BIAS_ONE) * m1 * inverse
            out_one[c] = m1.astype(jnp.bfloat16)
            out_two[c] = m2.astype(jnp.bfloat16)
        for copy in chunk(i):
            copy.start()
        return carry

    lax.fori_loop(0, 64 // block, run, 0)
    for i in range(64 // block):
        for copy in chunk(i):
            copy.wait()
    move.wait()


def per_device(state, damping, mask, gain, weight, spectral, moment_one, moment_two):
    own, near, pick, regrid, forward, inverse, along_x = tables()
    f32, bf16 = jnp.float32, jnp.bfloat16
    vmem = pl.BlockSpec(memory_space=pltpu.VMEM)
    hbm = pl.BlockSpec(memory_space=pltpu.HBM)
    anywhere = pl.BlockSpec(memory_space=pl.ANY)
    spec_t = jnp.transpose(spectral, (1, 2, 0))
    dma = pltpu.SemaphoreType.DMA
    new_state, coef_all, grad_all = pl.pallas_call(
        step_kernel,
        out_shape=(
            jax.ShapeDtypeStruct((1000, 128), f32),
            jax.ShapeDtypeStruct((ZPEERS, 64, 128), f32),
            jax.ShapeDtypeStruct((ZPEERS, 64, 128), f32),
        ),
        in_specs=[hbm] * 13,
        out_specs=(vmem, vmem, vmem),
        scratch_shapes=[
            pltpu.VMEM((1000, 128), f32),
            pltpu.VMEM((1, 256), f32),
            pltpu.VMEM((1, 256), jnp.int32),
            pltpu.VMEM((1, 64), f32),
            pltpu.VMEM((1, 64), f32),
            pltpu.VMEM((192, 512), f32),
            pltpu.VMEM((64, 128), f32),
            pltpu.SMEM((2048,), f32),
            pltpu.VMEM((512, 512), f32),
            pltpu.VMEM((512, 192), f32),
            pltpu.VMEM((64, 64, 128), f32),
            pltpu.VMEM((4096, 256), bf16),
            pltpu.VMEM((16, 256, 256), bf16),
            pltpu.VMEM((512, 256), f32),
            pltpu.VMEM((512, 256), f32),
            pltpu.VMEM((2, 192, 256), f32),
            pltpu.VMEM((2, 2, 32, 256), f32),
            pltpu.VMEM((192, 256), f32),
            pltpu.VMEM((1, 256), f32),
            pltpu.VMEM((64, 256), f32),
            pltpu.VMEM((64, 256), f32),
            pltpu.VMEM((64, 256), f32),
            pltpu.VMEM((64, 256), f32),
            pltpu.VMEM((256, 512), bf16),
            pltpu.VMEM((256, 512), bf16),
            pltpu.VMEM((2, 256, 256), f32),
            pltpu.VMEM((2, 256, 256), f32),
            pltpu.VMEM((2, 2, 2, 128, 128), f32),
            pltpu.VMEM((2, 2, 128, 128), f32),
            pltpu.VMEM((2, 2, CHIPS, 32, 128), f32),
            pltpu.VMEM((2, 2, CHIPS, 32, 128), f32),
            pltpu.VMEM((2, 2, 32, 128), f32),
            pltpu.VMEM((2, CHIPS, 64, 128), bf16),
            pltpu.VMEM((2, 256, 128), f32),
            pltpu.VMEM((256, 256), bf16),
            pltpu.VMEM((256, 256), bf16),
            dma((17,)),
            dma((2, 2)),
            dma((2, 2)),
            dma((2, 2)),
            dma((2, 2)),
            dma((2, 2, CHIPS)),
            dma((2, 2, CHIPS)),
            dma((CHIPS,)),
            dma((CHIPS,)),
            dma((CHIPS,)),
            dma((CHIPS,)),
            dma((2, 2, ZPEERS)),
            dma((2, 2, ZPEERS)),
        ],
        compiler_params=pltpu.CompilerParams(
            collective_id=0, has_side_effects=True, vmem_limit_bytes=40 * 1024 * 1024
        ),
        name="step",
    )(
        *(
            pltpu.with_memory_space_constraint(v, pltpu.HBM)
            for v in (
                state.reshape(1000, 128), damping, mask, gain.reshape(1, 64), weight.reshape(1, 64),
                pick, regrid, along_x, own, near, spec_t, forward, inverse,
            )
        )
    )
    new_spec, new_one, new_two, new_state = pl.pallas_call(
        update_kernel,
        out_shape=(
            jax.ShapeDtypeStruct((64, 64, 128), f32),
            jax.ShapeDtypeStruct((64, 64, 128), bf16),
            jax.ShapeDtypeStruct((64, 64, 128), bf16),
            jax.ShapeDtypeStruct((1000, 128), f32),
        ),
        in_specs=[vmem] * 5 + [anywhere],
        out_specs=(anywhere,) * 4,
        scratch_shapes=[
            pltpu.VMEM((64, 64, 128), f32),
            pltpu.VMEM((64, 64, 128), bf16),
            pltpu.VMEM((64, 64, 128), bf16),
            dma((8, 4)),
        ],
        compiler_params=pltpu.CompilerParams(vmem_limit_bytes=16 * 1024 * 1024),
        name="update",
    )(
        coef_all, grad_all, spec_t,
        jnp.transpose(moment_one, (1, 2, 0)), jnp.transpose(moment_two, (1, 2, 0)), new_state,
    )
    back = (2, 0, 1)
    return (
        new_state.reshape(state.shape),
        jnp.transpose(new_spec, back),
        jnp.transpose(new_one, back),
        jnp.transpose(new_two, back),
    )


def solution(mesh):
    in_specs = (
        P(("grp", "gy"), None, None, "gx", None),
        P("gx", None),
        P("gx", None),
        P(),
        P(),
        P("gx", None, None),
        P("gx", None, None),
        P("gx", None, None),
    )
    out_specs = (
        P(("grp", "gy"), None, None, "gx", None),
        P("gx", None, None),
        P("gx", None, None),
        P("gx", None, None),
    )
    return jax.shard_map(
        per_device, mesh=mesh, in_specs=in_specs, out_specs=out_specs, check_vma=False
    )
```

time: 81.6 us -> 60.9 us (0.75)
  local copies, waits for them, and re-layouts: 14 us -> 0.01 us
  Pallas kernels: 66.1 us -> 60.1 us
    unnamed x31 -> x6, local copies, waits for them, and re-layouts: 14 us -> 0.01 us
    pallas_call x1, Pallas kernels: 61.2 us -> 56.3 us  [per_device(): pl.pallas_call(step_kernel, out_shape=(jax.ShapeDtypeStruct((1000, 128),...]
    pallas_call x1, Pallas kernels: 4.88 us -> 3.82 us  [per_device(): pl.pallas_call(update_kernel, out_shape=(jax.ShapeDtypeStruct((64, 64, 12...]
where the time goes in v1:
time: 60.9 us; the launch traced here: 60.8 us
  Pallas kernels  60.1 us (99%)
  between operations  0.69 us (1%)
    pallas_call x1, Pallas kernels, per_device(): pl.pallas_call(step_kernel, out_shape=(jax.ShapeDtypeStruct((1000, 128),...  56.3 us
    pallas_call x1, Pallas kernels, per_device(): pl.pallas_call(update_kernel, out_shape=(jax.ShapeDtypeStruct((64, 64, 12...  3.82 us

profile of v1, /device:TPU:1, one launch (start us, length us, event | category | flops | bytes accessed | tf_op | source)
XLA Modules:
  0.0 60.8 jit_solution(17183975056972664015)
XLA Ops:
  0.6 0.0 copy-start
  0.6 0.0 copy-start.1
  0.7 0.0 copy-start.2
  0.7 56.3 %step.1 = (f32[1000,128]{1,0:T(8,128)S(1)}, f32[8,64,128]{2,1,0:T(8,128)S(1)}, f32[8,64,128]{2,1,0:T(8,128)S(1)}) custom-call(f32[1000,128]{1,0:T(8,128)} %bitcast.14, f32[1,256]{1,0:T(1,128)} %damping_h.1, s32[1,256]{1,0:T(1,128)} %mask_h.1, f32[1,64]{1,0:T(1,128)} %bitcast.15, f32[1,64]{1,0:T(1,128)} %bitcast.16, f32[192,512]{1,0:T(8,128)} %constant.17.clone.pick_h, ...), custom_call_target="tpu_custom_call" | custom-call | tf_op jit(solution)/shard_map/step/pallas_call | solution.py:576
  56.9 0.0 copy-done
  56.9 0.0 copy-done.1
  57.0 0.0 copy-done.2
  57.0 3.8 %update.1 = (f32[64,64,128]{2,1,0:T(8,128)}, bf16[64,64,128]{2,1,0:T(8,128)(2,1)}, bf16[64,64,128]{2,1,0:T(8,128)(2,1)}, f32[1000,128]{1,0:T(8,128)}) custom-call(f32[8,64,128]{2,1,0:T(8,128)S(1)} %get-tuple-element.11.coef, f32[8,64,128]{2,1,0:T(8,128)S(1)} %get-tuple-element.12.grad, f32[64,64,128]{2,1,0:T(8,128)S(1)} %bitcast.11, ...), custom_call_target="tpu_custom_call" | custom-call | tf_op jit(solution)/shard_map/update/pallas_call | solution.py:649
Async XLA Ops:
  0.6 56.3 %copy-start = (f32[128,64,64]{0,2,1:T(8,128)S(1)}, f32[128,64,64]{0,2,1:T(8,128)}, u32[]{:S(2)}) copy-start(f32[128,64,64]{0,2,1:T(8,128)} %param.20) | copy-start | bytes 6291460
  0.6 56.3 %copy-start.1 = (bf16[128,64,64]{0,2,1:T(8,128)(2,1)S(1)}, bf16[128,64,64]{0,2,1:T(8,128)(2,1)}, u32[]{:S(2)}) copy-start(bf16[128,64,64]{0,2,1:T(8,128)(2,1)} %param.21) | copy-start | bytes 3145732
  0.7 56.3 %copy-start.2 = (bf16[128,64,64]{0,2,1:T(8,128)(2,1)S(1)}, bf16[128,64,64]{0,2,1:T(8,128)(2,1)}, u32[]{:S(2)}) copy-start(bf16[128,64,64]{0,2,1:T(8,128)(2,1)} %param.22) | copy-start | bytes 3145732

commit v2 on v1

--- a/solution.py
+++ b/solution.py
@@ -13,6 +13,7 @@
 KM = 16
 CHIPS = 16
 ZPEERS = 8
+PIECES = (((0, 64),), ((0, 32), (32, 32)))
 TIME_STEP = 0.02
 FACE_GAIN = 10.0
 LOSS_SCALE = 1.0 / 2048.0
@@ -127,16 +128,8 @@
     return own, near, pick, regrid, forward, inverse, along_x
 
 
-def normal_tail(x):
-    bell = jnp.exp2(x * x * (-0.5 * LOG2E))
-    den = 1.0 + (0.3275911 * HALF_ROOT) * jnp.abs(x)
-    t = pl.reciprocal(den, approx=True)
-    t = t * (2.0 - den * t)
-    poly = 0.5 * 1.061405429 * t - 0.5 * 1.453152027
-    poly = poly * t + 0.5 * 1.421413741
-    poly = poly * t - 0.5 * 0.284496736
-    poly = poly * t + 0.5 * 0.254829592
-    return poly * t * bell, bell
+def normal_cdf(x):
+    return 0.5 + 0.5 * lax.erf(x * HALF_ROOT)
 
 
 def dot_f32(a, b):
@@ -261,47 +254,64 @@
             device_id_type=MESH,
         )
 
-    def part_copy(phase, r, k):
+    def piece(phase, n):
+        first, count = PIECES[phase][n]
+        return first, count, pl.ds(first, count)
+
+    def part_copy(phase, n, k):
+        rows = piece(phase, n)[2]
         return pltpu.make_async_remote_copy(
-            src_ref=parts.at[phase, r, k],
-            dst_ref=inbox.at[phase, r, k],
-            send_sem=part_s.at[phase, r, k],
-            recv_sem=part_r.at[phase, r, k],
+            src_ref=parts.at[phase, k, rows],
+            dst_ref=inbox.at[phase, k, rows],
+            send_sem=part_s.at[phase, n, k],
+            recv_sem=part_r.at[phase, n, k],
             device_id={"gx": 2 * chip_at(k, 1) + core},
             device_id_type=MESH,
         )
 
-    def expand(phase, r, k):
-        base = chip_at(k, 1) * 128 + 8 * chip
-        acc = jnp.zeros((32, 128), jnp.float32)
-        for m in range(4):
-            rows = pl.ds(32 * m, 32)
-            acc = acc + table_x[base + 4 * core + m] * fwd_sum[phase, core, r, rows, :]
-            acc = acc + table_x[base + 4 - 4 * core + m] * sib_sum[phase, r, rows, :]
-        return acc
-
-    def scatter(phase, r):
-        sib_copy(phase, r).wait()
+    def expand(phase, n, k, whose):
+        base = chip_at(k, 1) * 128 + 8 * chip + (4 * core if whose == 0 else 4 - 4 * core)
+        first, count, unused = piece(phase, n)
+        sums = []
+        for r in range(first // 32, -(-(first + count) // 32)):
+            acc = jnp.zeros((32, 128), jnp.float32)
+            for m in range(4):
+                rows = pl.ds(32 * m, 32)
+                value = (
+                    fwd_sum[phase, core, r, rows, :] if whose == 0 else sib_sum[phase, r, rows, :]
+                )
+                acc = acc + table_x[base + m] * value
+            sums.append(acc)
+        return sums[0] if len(sums) == 1 else jnp.concatenate(sums, axis=0)
+
+    def prepare(phase, n):
+        rows = piece(phase, n)[2]
+        for k in (*far, 0):
+            parts[phase, k, rows, :] = expand(phase, n, k, 0)
+
+    def scatter(phase, n):
+        rows = piece(phase, n)[2]
         for k in far:
-            parts[phase, r, k] = expand(phase, r, k)
-            part_copy(phase, r, k).start()
-        total[phase, r] = expand(phase, r, 0)
-
-    def gather_sum(phase, r):
+            parts[phase, k, rows, :] += expand(phase, n, k, 1)
+            part_copy(phase, n, k).start()
+        total[phase, rows, :] = parts[phase, 0, rows, :] + expand(phase, n, 0, 1)
+
+    def gather_sum(phase, n):
+        rows = piece(phase, n)[2]
         ref = (coef_all, grad_all)[phase]
-        summed = total[phase, r]
+        summed = total[phase, rows, :]
         for k in others:
-            part_copy(phase, r, k).wait_recv()
-            summed = summed + inbox[phase, r, k]
-        ref[pl.ds(zme, 1), pl.ds(32 * r, 32), :] = summed[None]
-
-    def z_copy(phase, r, k):
-        ref = (coef_all, grad_all)[phase].at[zme, pl.ds(32 * r, 32)]
+            part_copy(phase, n, k).wait_recv()
+            summed = summed + inbox[phase, k, rows, :]
+        ref[pl.ds(zme, 1), rows, :] = summed[None]
+
+    def z_copy(phase, n, k):
+        ref = (coef_all, grad_all)[phase].at[zme, piece(phase, n)[2]]
         return pltpu.make_async_remote_copy(
             src_ref=ref,
             dst_ref=ref,
-            send_sem=z_s.at[phase, r, k],
-            recv_sem=z_r.at[phase, r, k],
+            send_sem=z_s.at[phase, n, k],
+            recv_sem=z_r.at[phase, n, k],
             device_id=z_at(k),
             device_id_type=MESH,
         )
@@ -319,7 +329,7 @@
             row = a[pl.ds(m * 16 + j, 1), :]
             for r in range(2):
                 x = gcol[pl.ds(32 * r, 32), :] * row
-                lifted = jnp.maximum(x, 0.0) - jnp.abs(x) * normal_tail(x)[0]
+                lifted = x * normal_cdf(x)
                 g[rows_of(m, r), 256 * side : 256 * side + 256] = lifted.astype(jnp.bfloat16)
 
     for i in range(4):
@@ -340,6 +350,7 @@
 
     for r in range(2):
         sib_copy(0, r).start()
+
     lanes = lax.broadcasted_iota(jnp.int32, (32, 256), 1)
     ez = lax.rem(lanes, 16)
 
@@ -364,19 +375,22 @@
     q[128:500, 128:256] = state[pl.ds(257, 372, stride=2), :]
     q[500:512, :] = jnp.zeros((12, 256), jnp.float32)
     sink[...] = mask[...].astype(jnp.float32) * damping[...]
-    faces[0] = dot_f32(pick[...], q[...])
+    faces[0, 0:64] = dot_f32(pick[0:64, :], q[...])
     for side in range(2):
         halo_copy(0, side).start()
+    prepare(0, 0)
     for r in range(2):
-        scatter(0, r)
+        sib_copy(0, r).wait()
+    scatter(0, 0)
+    faces[0, 64:192] = dot_f32(pick[64:192, :], q[...])
 
     sec[...] = q[...] + TIME_STEP * rates(0, q)
     faces[1] = dot_f32(pick[...], sec[...])
     for side in range(2):
         halo_copy(1, side).start()
 
-    for r in range(2):
-        gather_sum(0, r)
+    for n in range(len(PIECES[0])):
+        gather_sum(0, n)
 
     loads[14].wait()
 
@@ -415,9 +429,9 @@
         if hops(k) > 2:
             hop_copy(k).start()
     hop_copy(0).start()
-    for r in range(2):
+    for n in range(len(PIECES[0])):
         for k in z_far:
-            z_copy(0, r, k).start()
+            z_copy(0, n, k).start()
 
     done = 0.5 * (q[...] + sec[...] + TIME_STEP * rates(1, sec))
     new_state[pl.ds(0, 500, stride=2), :] = done[0:500, 0:128]
@@ -469,8 +483,8 @@
             for r in range(2):
                 rows = rows_of(m, r)
                 x = pre[slot, rows, :]
-                tail, bell = normal_tail(x)
-                cdf = jnp.where(x >= 0.0, 1.0 - tail, tail)
+                cdf = normal_cdf(x)
+                bell = jnp.exp2(x * x * (-0.5 * LOG2E))
                 slope[slot, rows, :] = cdf + x * bell * GAUSS_NORM
                 act = x * cdf * wcol[pl.ds(32 * r, 32), :]
                 acc = acc + jnp.sum(act.reshape(4, 8, 256), axis=0)
@@ -499,17 +513,20 @@
 
     for r in range(2):
         sib_copy(1, r).start()
-    for r in range(2):
-        scatter(1, r)
-    for r in range(2):
-        gather_sum(1, r)
+    for n in range(2):
+        prepare(1, n)
+    for n in range(2):
+        sib_copy(1, n).wait()
+        scatter(1, n)
+    for n in range(len(PIECES[1])):
+        gather_sum(1, n)
         for k in z_far:
-            z_copy(1, r, k).start()
+            z_copy(1, n, k).start()
 
     for k in others:
         for phase in range(2):
-            for r in range(2):
-                part_copy(phase, r, k).wait_send()
+            for n in range(len(PIECES[phase])):
+                part_copy(phase, n, k).wait_send()
         mix_copy(k).wait_send()
     for k in range(CHIPS):
         hop_copy(k).wait_send()
@@ -517,9 +534,9 @@
         for side in range(2):
             halo_copy(stage, side).wait_send()
     for phase in range(2):
-        for r in range(2):
+        for n in range(len(PIECES[phase])):
             for k in z_far:
-                z_copy(phase, r, k).wait()
+                z_copy(phase, n, k).wait()
 
 
 def update_kernel(
@@ -549,8 +566,7 @@
             m2 = BETA_TWO * two[c].astype(jnp.float32) + (1.0 - BETA_TWO) * acc * acc
             scaled = m2 * (1.0 / BIAS_TWO)
             den = scaled * lax.rsqrt(scaled) + EPSILON
-            inverse = pl.reciprocal(den, approx=True)
-            inverse = inverse * (2.0 - den * inverse)
+            inverse = 1.0 / den
             out_spec[c] = spec[c] - (LEARN_RATE / BIAS_ONE) * m1 * inverse
             out_one[c] = m1.astype(jnp.bfloat16)
             out_two[c] = m2.astype(jnp.bfloat16)
@@ -612,9 +628,9 @@
             pltpu.VMEM((2, 256, 256), f32),
             pltpu.VMEM((2, 2, 2, 128, 128), f32),
             pltpu.VMEM((2, 2, 128, 128), f32),
-            pltpu.VMEM((2, 2, CHIPS, 32, 128), f32),
-            pltpu.VMEM((2, 2, CHIPS, 32, 128), f32),
-            pltpu.VMEM((2, 2, 32, 128), f32),
+            pltpu.VMEM((2, CHIPS, 64, 128), f32),
+            pltpu.VMEM((2, CHIPS, 64, 128), f32),
+            pltpu.VMEM((2, 64, 128), f32),
             pltpu.VMEM((2, CHIPS, 64, 128), bf16),
             pltpu.VMEM((2, 256, 128), f32),
             pltpu.VMEM((256, 256), bf16),

time: 60.9 us -> 55.7 us (0.915)
  Pallas kernels: 60.1 us -> 54.8 us
    pallas_call x1, Pallas kernels: 56.3 us -> 51.2 us  [per_device(): pl.pallas_call(step_kernel, out_shape=(jax.ShapeDtypeStruct((1000, 128),...]
where the time goes in v2:
time: 55.7 us; the launch traced here: 55.5 us
  Pallas kernels  54.8 us (98%)
  between operations  0.69 us (1%)
    pallas_call x1, Pallas kernels, per_device(): pl.pallas_call(step_kernel, out_shape=(jax.ShapeDtypeStruct((1000, 128),...  51.2 us
    pallas_call x1, Pallas kernels, per_device(): pl.pallas_call(update_kernel, out_shape=(jax.ShapeDtypeStruct((64, 64, 12...  3.59 us

profile of v2, /device:TPU:1, one launch (start us, length us, event | category | flops | bytes accessed | tf_op | source)
XLA Modules:
  0.0 55.5 jit_solution(7028980505355788585)
XLA Ops:
  0.6 0.0 copy-start
  0.6 0.0 copy-start.1
  0.7 0.0 copy-start.2
  0.7 51.2 %step.1 = (f32[1000,128]{1,0:T(8,128)S(1)}, f32[8,64,128]{2,1,0:T(8,128)S(1)}, f32[8,64,128]{2,1,0:T(8,128)S(1)}) custom-call(f32[1000,128]{1,0:T(8,128)} %bitcast.14, f32[1,256]{1,0:T(1,128)} %damping_h.1, s32[1,256]{1,0:T(1,128)} %mask_h.1, f32[1,64]{1,0:T(1,128)} %bitcast.15, f32[1,64]{1,0:T(1,128)} %bitcast.16, f32[192,512]{1,0:T(8,128)} %constant.17.clone.pick_h, ...), custom_call_target="tpu_custom_call" | custom-call | tf_op jit(solution)/shard_map/step/pallas_call | solution.py:592
  51.9 0.0 copy-done
  51.9 0.0 copy-done.1
  51.9 0.0 copy-done.2
  51.9 3.6 %update.1 = (f32[64,64,128]{2,1,0:T(8,128)}, bf16[64,64,128]{2,1,0:T(8,128)(2,1)}, bf16[64,64,128]{2,1,0:T(8,128)(2,1)}, f32[1000,128]{1,0:T(8,128)}) custom-call(f32[8,64,128]{2,1,0:T(8,128)S(1)} %get-tuple-element.11.coef, f32[8,64,128]{2,1,0:T(8,128)S(1)} %get-tuple-element.12.grad, f32[64,64,128]{2,1,0:T(8,128)S(1)} %bitcast.11, ...), custom_call_target="tpu_custom_call" | custom-call | tf_op jit(solution)/shard_map/update/pallas_call | solution.py:665
Async XLA Ops:
  0.6 51.2 %copy-start = (f32[128,64,64]{0,2,1:T(8,128)S(1)}, f32[128,64,64]{0,2,1:T(8,128)}, u32[]{:S(2)}) copy-start(f32[128,64,64]{0,2,1:T(8,128)} %param.20) | copy-start | bytes 6291460
  0.6 51.2 %copy-start.1 = (bf16[128,64,64]{0,2,1:T(8,128)(2,1)S(1)}, bf16[128,64,64]{0,2,1:T(8,128)(2,1)}, u32[]{:S(2)}) copy-start(bf16[128,64,64]{0,2,1:T(8,128)(2,1)} %param.21) | copy-start | bytes 3145732
  0.7 51.2 %copy-start.2 = (bf16[128,64,64]{0,2,1:T(8,128)(2,1)S(1)}, bf16[128,64,64]{0,2,1:T(8,128)(2,1)}, u32[]{:S(2)}) copy-start(bf16[128,64,64]{0,2,1:T(8,128)(2,1)} %param.22) | copy-start | bytes 3145732

commit v3 on v2

--- a/solution.py
+++ b/solution.py
@@ -151,11 +151,11 @@
 def step_kernel(
     state_h, damping_h, mask_h, gain_h, weight_h, pick_h, regrid_h, table_h, own_h, near_h, spec_h,
     fwd_h, inv_h,
-    new_state, coef_all, grad_all,
+    new_state, coef_all, grad_all, half_grad,
     state, damping, mask, gain, weight, pick, regrid, table_x, own, near, spec, fwd, inv,
     q, sec, faces, halo, edge, sink, a, b, gcol, wcol, g_a, g_b, pre, slope,
     fwd_sum, sib_sum, parts, inbox, total, mixed,
-    ax, ax_hi, ax_lo,
+    ax, ax_parts,
     load_sem, halo_s, halo_r, sib_s, sib_r, part_s, part_r, mix_s, mix_r, hop_s, hop_r, z_s, z_r,
 ):
     grp, gx, gy = lax.axis_index("grp"), lax.axis_index("gx"), lax.axis_index("gy")
@@ -201,7 +201,8 @@
         (near_h, near),
         (spec_h, spec),
         (weight_h, weight),
-        (inv_h, inv),
+        (inv_h, inv.at[:, pl.ds(0, 256)]),
+        (inv_h, inv.at[:, pl.ds(256, 256)]),
     ]
     loads = [pltpu.make_async_copy(*m, load_sem.at[i]) for i, m in enumerate(moves)]
     for c in loads[:7]:
@@ -221,7 +222,7 @@
 
     for c in loads[:3]:
         c.wait()
-    for c in loads[7:]:
+    for c in loads[7:12]:
         c.start()
     q[0:128, 0:128] = state[pl.ds(0, 128, stride=2), :]
     q[0:128, 128:256] = state[pl.ds(1, 128, stride=2), :]
@@ -332,19 +333,20 @@
                 lifted = x * normal_cdf(x)
                 g[rows_of(m, r), 256 * side : 256 * side + 256] = lifted.astype(jnp.bfloat16)
 
-    for i in range(4):
-        loads[3 + i].wait()
-
     def lift_four(i):
+        part = pl.ds(pl.multiple_of(1024 * i, 1024), 1024)
+        pltpu.make_async_copy(fwd_h.at[part], fwd.at[part], load_sem.at[3 + i]).wait()
         lift(4 * i, g_a, 0)
         lift(4 * i + 1, g_a, 1)
-        transform(0, lax.rem(2 * i + 7, 8), g_b, (0, 1))
+        transform(0, jnp.maximum(2 * i - 1, 0), g_b, (0, 1))
         lift(4 * i + 2, g_b, 0)
         lift(4 * i + 3, g_b, 1)
         transform(0, 2 * i, g_a, (0, 1))
 
     each(0, 4, lift_four)
     transform(0, 7, g_b, (0, 1))
+    for c in loads[12:]:
+        c.start()
 
     pl.semaphore_wait(barrier, CHIPS - 1 + 2 + ZPEERS - 1)
 
@@ -369,7 +371,7 @@
         rate = dot_f32(own[...], fields[...]) + dot_f32(near[...], edge[...])
         return rate - sink[...] * fields[...]
 
-    for c in loads[7:14]:
+    for c in loads[7:12]:
         c.wait()
     q[128:500, 0:128] = state[pl.ds(256, 372, stride=2), :]
     q[128:500, 128:256] = state[pl.ds(257, 372, stride=2), :]
@@ -384,6 +386,8 @@
     scatter(0, 0)
     faces[0, 64:192] = dot_f32(pick[64:192, :], q[...])
 
+    for c in loads[12:14]:
+        c.wait()
     sec[...] = q[...] + TIME_STEP * rates(0, q)
     faces[1] = dot_f32(pick[...], sec[...])
     for side in range(2):
@@ -463,18 +467,18 @@
     for half in range(2):
         value = ax[half]
         high = value.astype(jnp.bfloat16)
-        ax_hi[:, 128 * half : 128 * half + 128] = high
-        ax_lo[:, 128 * half : 128 * half + 128] = (value - high.astype(jnp.float32)).astype(
-            jnp.bfloat16
-        )
+        low = (value - high.astype(jnp.float32)).astype(jnp.bfloat16)
+        ax_parts[:, 128 * half : 128 * half + 128] = high
+        ax_parts[:, 256 + 128 * half : 384 + 128 * half] = low
 
     loads[15].wait()
     loads[16].wait()
+    loads[17].wait()
     wcol[...] = column(weight[...])
     g_b[...] = jnp.zeros_like(g_b)
 
     def inverse(j, slot):
-        pre[slot] = dot_bf16(ax_hi[...], inv[j]) + dot_bf16(ax_lo[...], inv[j])
+        pre[slot] = dot_bf16(ax_parts[...], inv[j])
 
     def back(j, slot, g, side):
         cols = slice(256 * side, 256 * side + 256)
@@ -533,14 +537,26 @@
     for stage in range(2):
         for side in range(2):
             halo_copy(stage, side).wait_send()
-    for phase in range(2):
-        for n in range(len(PIECES[phase])):
-            for k in z_far:
-                z_copy(phase, n, k).wait()
+    for k in z_far:
+        z_copy(0, 0, k).wait_recv()
+        z_copy(1, 0, k).wait_recv()
+
+    def first_half(c):
+        acc = coef_all[0, pl.ds(c, 1), :] * grad_all[0, 0:32, :]
+        for t in range(1, ZPEERS):
+            acc = acc + coef_all[t, pl.ds(c, 1), :] * grad_all[t, 0:32, :]
+        half_grad[pl.ds(c, 1)] = acc[None]
+
+    each(0, 64, first_half, unroll=8)
+
+    for k in z_far:
+        z_copy(1, 1, k).wait()
+        z_copy(0, 0, k).wait_send()
+        z_copy(1, 0, k).wait_send()
 
 
 def update_kernel(
-    coef, grad, spec, one, two, state, new_spec, new_one, new_two, new_state,
+    coef, grad, half, spec, one, two, state, new_spec, new_one, new_two, new_state,
     out_spec, out_one, out_two, sem,
 ):
     move = pltpu.make_async_copy(state, new_state, sem.at[0, 3])
@@ -559,9 +575,10 @@
     def run(i, carry):
         for n in range(block):
             c = block * i + n
-            acc = coef[0, pl.ds(c, 1), :] * grad[0]
+            acc = coef[0, pl.ds(c, 1), :] * grad[0, 32:64, :]
             for t in range(1, ZPEERS):
-                acc = acc + coef[t, pl.ds(c, 1), :] * grad[t]
+                acc = acc + coef[t, pl.ds(c, 1), :] * grad[t, 32:64, :]
+            acc = jnp.concatenate([half[c], acc], axis=0)
             m1 = BETA_ONE * one[c].astype(jnp.float32) + (1.0 - BETA_ONE) * acc
             m2 = BETA_TWO * two[c].astype(jnp.float32) + (1.0 - BETA_TWO) * acc * acc
             scaled = m2 * (1.0 / BIAS_TWO)
@@ -589,15 +606,16 @@
     anywhere = pl.BlockSpec(memory_space=pl.ANY)
     spec_t = jnp.transpose(spectral, (1, 2, 0))
     dma = pltpu.SemaphoreType.DMA
-    new_state, coef_all, grad_all = pl.pallas_call(
+    new_state, coef_all, grad_all, half_grad = pl.pallas_call(
         step_kernel,
         out_shape=(
             jax.ShapeDtypeStruct((1000, 128), f32),
             jax.ShapeDtypeStruct((ZPEERS, 64, 128), f32),
             jax.ShapeDtypeStruct((ZPEERS, 64, 128), f32),
+            jax.ShapeDtypeStruct((64, 32, 128), f32),
         ),
         in_specs=[hbm] * 13,
-        out_specs=(vmem, vmem, vmem),
+        out_specs=(vmem,) * 4,
         scratch_shapes=[
             pltpu.VMEM((1000, 128), f32),
             pltpu.VMEM((1, 256), f32),
@@ -611,7 +629,7 @@
             pltpu.VMEM((512, 192), f32),
             pltpu.VMEM((64, 64, 128), f32),
             pltpu.VMEM((4096, 256), bf16),
-            pltpu.VMEM((16, 256, 256), bf16),
+            pltpu.VMEM((16, 512, 256), bf16),
             pltpu.VMEM((512, 256), f32),
             pltpu.VMEM((512, 256), f32),
             pltpu.VMEM((2, 192, 256), f32),
@@ -633,9 +651,8 @@
             pltpu.VMEM((2, 64, 128), f32),
             pltpu.VMEM((2, CHIPS, 64, 128), bf16),
             pltpu.VMEM((2, 256, 128), f32),
-            pltpu.VMEM((256, 256), bf16),
-            pltpu.VMEM((256, 256), bf16),
-            dma((17,)),
+            pltpu.VMEM((256, 512), bf16),
+            dma((18,)),
             dma((2, 2)),
             dma((2, 2)),
             dma((2, 2)),
@@ -670,7 +687,7 @@
             jax.ShapeDtypeStruct((64, 64, 128), bf16),
             jax.ShapeDtypeStruct((1000, 128), f32),
         ),
-        in_specs=[vmem] * 5 + [anywhere],
+        in_specs=[vmem] * 6 + [anywhere],
         out_specs=(anywhere,) * 4,
         scratch_shapes=[
             pltpu.VMEM((64, 64, 128), f32),
@@ -681,7 +698,7 @@
         compiler_params=pltpu.CompilerParams(vmem_limit_bytes=16 * 1024 * 1024),
         name="update",
     )(
-        coef_all, grad_all, spec_t,
+        coef_all, grad_all, half_grad, spec_t,
         jnp.transpose(moment_one, (1, 2, 0)), jnp.transpose(moment_two, (1, 2, 0)), new_state,
     )
     back = (2, 0, 1)

time: 55.7 us -> 54.2 us (0.973)
  Pallas kernels: 54.8 us -> 53.3 us
    pallas_call x1, Pallas kernels: 51.2 us -> 50.3 us  [per_device(): pl.pallas_call(step_kernel, out_shape=(jax.ShapeDtypeStruct((1000, 128),...]
    pallas_call x1, Pallas kernels: 3.59 us -> 3.03 us  [per_device(): pl.pallas_call(update_kernel, out_shape=(jax.ShapeDtypeStruct((64, 64, 12...]
where the time goes in v3:
time: 54.2 us; the launch traced here: 54 us
  Pallas kernels  53.3 us (98%)
  between operations  0.69 us (1%)
    pallas_call x1, Pallas kernels, per_device(): pl.pallas_call(step_kernel, out_shape=(jax.ShapeDtypeStruct((1000, 128),...  50.3 us
    pallas_call x1, Pallas kernels, per_device(): pl.pallas_call(update_kernel, out_shape=(jax.ShapeDtypeStruct((64, 64, 12...  3.03 us

profile of v3, /device:TPU:1, one launch (start us, length us, event | category | flops | bytes accessed | tf_op | source)
XLA Modules:
  0.0 54.0 jit_solution(15548449707612357117)
XLA Ops:
  0.6 0.0 copy-start
  0.6 0.0 copy-start.1
  0.7 0.0 copy-start.2
  0.7 50.3 %step.1 = (f32[1000,128]{1,0:T(8,128)S(1)}, f32[8,64,128]{2,1,0:T(8,128)S(1)}, f32[8,64,128]{2,1,0:T(8,128)S(1)}, f32[64,32,128]{2,1,0:T(8,128)S(1)}) custom-call(f32[1000,128]{1,0:T(8,128)} %bitcast.14, f32[1,256]{1,0:T(1,128)} %damping_h.1, s32[1,256]{1,0:T(1,128)} %mask_h.1, f32[1,64]{1,0:T(1,128)} %bitcast.15, f32[1,64]{1,0:T(1,128)} %bitcast.16, ...), custom_call_target="tpu_custom_call" | custom-call | tf_op jit(solution)/shard_map/step/pallas_call | solution.py:609
  50.9 0.0 copy-done
  51.0 0.0 copy-done.1
  51.0 0.0 copy-done.2
  51.0 3.0 %update.1 = (f32[64,64,128]{2,1,0:T(8,128)}, bf16[64,64,128]{2,1,0:T(8,128)(2,1)}, bf16[64,64,128]{2,1,0:T(8,128)(2,1)}, f32[1000,128]{1,0:T(8,128)}) custom-call(f32[8,64,128]{2,1,0:T(8,128)S(1)} %get-tuple-element.12.coef, f32[8,64,128]{2,1,0:T(8,128)S(1)} %get-tuple-element.13.grad, f32[64,32,128]{2,1,0:T(8,128)S(1)} %get-tuple-element.14.half, ...), custom_call_target="tpu_custom_call" | custom-call | tf_op jit(solution)/shard_map/update/pallas_call | solution.py:682
Async XLA Ops:
  0.6 50.3 %copy-start = (f32[128,64,64]{0,2,1:T(8,128)S(1)}, f32[128,64,64]{0,2,1:T(8,128)}, u32[]{:S(2)}) copy-start(f32[128,64,64]{0,2,1:T(8,128)} %param.20) | copy-start | bytes 6291460
  0.6 50.3 %copy-start.1 = (bf16[128,64,64]{0,2,1:T(8,128)(2,1)S(1)}, bf16[128,64,64]{0,2,1:T(8,128)(2,1)}, u32[]{:S(2)}) copy-start(bf16[128,64,64]{0,2,1:T(8,128)(2,1)} %param.21) | copy-start | bytes 3145732
  0.7 50.3 %copy-start.2 = (bf16[128,64,64]{0,2,1:T(8,128)(2,1)S(1)}, bf16[128,64,64]{0,2,1:T(8,128)(2,1)}, u32[]{:S(2)}) copy-start(bf16[128,64,64]{0,2,1:T(8,128)(2,1)} %param.22) | copy-start | bytes 3145732

commit v4 on v3

--- a/solution.py
+++ b/solution.py
@@ -418,7 +418,7 @@
         )
 
     def hop_copy(k):
-        direct = hops(k) > 2
+        direct = hops(k) > 3
         return pltpu.make_async_remote_copy(
             src_ref=mixed.at[0, 0 if direct else k],
             dst_ref=mixed.at[1, k],
@@ -430,7 +430,7 @@
 
     for k in far:
         mix_copy(k).start()
-        if hops(k) > 2:
+        if hops(k) > 3:
             hop_copy(k).start()
     hop_copy(0).start()
     for n in range(len(PIECES[0])):
@@ -451,7 +451,7 @@
     sums = add_modes(0, 0, zeros)
     for k in others:
         mix_copy(k).wait_recv()
-        if hops(k) <= 2:
+        if hops(k) <= 3:
             hop_copy(k).start()
         sums = add_modes(0, k, sums)
     for m in range(4):

time: 54.2 us -> 53.8 us (level)
  no operation moved by 1% of the time
where the time goes in v4:
time: 53.8 us; the launch traced here: 53.7 us
  Pallas kernels  53 us (99%)
  between operations  0.69 us (1%)
    pallas_call x1, Pallas kernels, per_device(): pl.pallas_call(step_kernel, out_shape=(jax.ShapeDtypeStruct((1000, 128),...  50 us
    pallas_call x1, Pallas kernels, per_device(): pl.pallas_call(update_kernel, out_shape=(jax.ShapeDtypeStruct((64, 64, 12...  3.03 us

profile of v4, /device:TPU:1, one launch (start us, length us, event | category | flops | bytes accessed | tf_op | source)
XLA Modules:
  0.0 53.7 jit_solution(4941270410804080480)
XLA Ops:
  0.6 0.0 copy-start
  0.6 0.0 copy-start.1
  0.7 0.0 copy-start.2
  0.7 50.0 %step.1 = (f32[1000,128]{1,0:T(8,128)S(1)}, f32[8,64,128]{2,1,0:T(8,128)S(1)}, f32[8,64,128]{2,1,0:T(8,128)S(1)}, f32[64,32,128]{2,1,0:T(8,128)S(1)}) custom-call(f32[1000,128]{1,0:T(8,128)} %bitcast.14, f32[1,256]{1,0:T(1,128)} %damping_h.1, s32[1,256]{1,0:T(1,128)} %mask_h.1, f32[1,64]{1,0:T(1,128)} %bitcast.15, f32[1,64]{1,0:T(1,128)} %bitcast.16, ...), custom_call_target="tpu_custom_call" | custom-call | tf_op jit(solution)/shard_map/step/pallas_call | solution.py:609
  50.6 0.0 copy-done
  50.6 0.0 copy-done.1
  50.6 0.0 copy-done.2
  50.7 3.0 %update.1 = (f32[64,64,128]{2,1,0:T(8,128)}, bf16[64,64,128]{2,1,0:T(8,128)(2,1)}, bf16[64,64,128]{2,1,0:T(8,128)(2,1)}, f32[1000,128]{1,0:T(8,128)}) custom-call(f32[8,64,128]{2,1,0:T(8,128)S(1)} %get-tuple-element.12.coef, f32[8,64,128]{2,1,0:T(8,128)S(1)} %get-tuple-element.13.grad, f32[64,32,128]{2,1,0:T(8,128)S(1)} %get-tuple-element.14.half, ...), custom_call_target="tpu_custom_call" | custom-call | tf_op jit(solution)/shard_map/update/pallas_call | solution.py:682
Async XLA Ops:
  0.6 50.0 %copy-start = (f32[128,64,64]{0,2,1:T(8,128)S(1)}, f32[128,64,64]{0,2,1:T(8,128)}, u32[]{:S(2)}) copy-start(f32[128,64,64]{0,2,1:T(8,128)} %param.20) | copy-start | bytes 6291460
  0.6 50.0 %copy-start.1 = (bf16[128,64,64]{0,2,1:T(8,128)(2,1)S(1)}, bf16[128,64,64]{0,2,1:T(8,128)(2,1)}, u32[]{:S(2)}) copy-start(bf16[128,64,64]{0,2,1:T(8,128)(2,1)} %param.21) | copy-start | bytes 3145732
  0.7 50.0 %copy-start.2 = (bf16[128,64,64]{0,2,1:T(8,128)(2,1)S(1)}, bf16[128,64,64]{0,2,1:T(8,128)(2,1)}, u32[]{:S(2)}) copy-start(bf16[128,64,64]{0,2,1:T(8,128)(2,1)} %param.22) | copy-start | bytes 3145732
